TPU v7x, 32 devices: a whole 2x2x4 slice. The times are simulated.
32 devices in a mesh: groups: 2 (over y), seq: 4 (over z), rep: 2 (over x), fsdp: 2 (over core).
Axes of the slice: x: 2, y: 2, z: 4, core: 2. Of those that a mesh axis runs over, the one named last changes fastest.
Arguments:
- activations: bfloat16 [8, 512, 2048], P(('groups', 'rep', 'fsdp'), 'seq'), parts along dimension 0, may hold values from -6 to 6
- queries: bfloat16 [8, 512, 2048], P(('groups', 'rep', 'fsdp'), 'seq'), parts along dimension 0, may hold values from -102 to 102
- key_weight: bfloat16 [2048, 512], P(('seq', 'fsdp')), may hold values from -0.125 to 0.125
- value_weight: bfloat16 [2048, 512], P(('seq', 'fsdp')), may hold values from -0.125 to 0.125
- segment_ids: int32 [8, 512], P(('groups', 'rep', 'fsdp'), 'seq'), parts along dimension 0, may hold values from 0 to 3, never falling along the last dimension, each value on 1 to 384 neighbouring positions
- out_grad: bfloat16 [8, 512, 2048], P(('groups', 'rep', 'fsdp'), 'seq'), parts along dimension 0, may hold values from -6 to 6
Outputs:
- context: bfloat16 [8, 512, 2048], P(('groups', 'rep', 'fsdp'), 'seq'), parts along dimension 0
- query_grad: bfloat16 [8, 512, 2048], P(('groups', 'rep', 'fsdp'), 'seq'), parts along dimension 0
- input_grad: bfloat16 [8, 512, 2048], P(('groups', 'rep', 'fsdp'), 'seq'), parts along dimension 0
- key_weight_grad: bfloat16 [4096, 512], P(('groups', 'seq', 'fsdp')), parts along dimension 0
- value_weight_grad: bfloat16 [4096, 512], P(('groups', 'seq', 'fsdp')), parts along dimension 0
There are 2 independent parts, one for each index of `groups`. A program takes and returns all parts, laid end to end along the dimension named above; an argument that names none is the same for every part. Nothing has to cross between parts.
Inputs may be any that keep to these rules, and one draw needn't show every extreme that they name: `segment_ids`: document numbers never fall along a sequence; a document covers at most 384 positions.
All inputs are finite; a program needn't handle non-finite values.
Results may differ from a plain program's by a relative error of at most 0.025.
The roundings to bfloat16 on the way count: a program that leaves them out, or rounds other values in their place, can miss the bound.
Values may be sent and summed in bfloat16 or wider, within the bound.
No kernel may reach another device: no remote copies, remote signals or barrier semaphores. Data moves between devices by JAX's collectives and lax.ppermute only.
A program may use at most 64 MiB of HBM per device.

v0:
```python
import math
import jax
import jax.numpy as jnp
from jax import lax
from jax.sharding import PartitionSpec as P

HEADS = 16
KV_HEADS = 4
HEAD_DIM = 128
masked_low = -1e30


def block_mask(seg_all, row_start, col_start, block_width):
    row_pos = row_start + lax.iota(jnp.int32, block_width)
    col_pos = col_start + lax.iota(jnp.int32, block_width)
    seg_rows = lax.dynamic_slice_in_dim(seg_all, row_start, block_width)
    seg_cols = lax.dynamic_slice_in_dim(seg_all, col_start, block_width)
    return (col_pos[None, :] <= row_pos[:, None]) & (seg_cols[None, :] == seg_rows[:, None])


def block_scores(query_block, key_block, inv_root):
    return (
        jnp.einsum("qhd,khd->hqk", query_block, key_block, preferred_element_type=jnp.float32)
        * inv_root
    )


def take_block(source, index, block_width):
    return lax.dynamic_slice_in_dim(source, index * block_width, block_width, 0)


def attend(query_part, key_part, value_part, seg_all):
    length, heads_here, head_size = query_part.shape
    block_width = min(512, length)
    block_count = length // block_width
    inv_root = 1.0 / math.sqrt(head_size)

    def stats_row(i, log_totals):
        query_block = take_block(query_part, i, block_width)

        def stats_inner(j, state_now):
            running_max, running_sum = state_now
            scores = block_scores(query_block, take_block(key_part, j, block_width), inv_root)
            allowed = block_mask(seg_all, i * block_width, j * block_width, block_width)[None]
            scores = jnp.where(allowed, scores, masked_low)
            new_max = jnp.maximum(running_max, jnp.max(scores, axis=-1))
            weights = jnp.where(allowed, jnp.exp(scores - new_max[..., None]), 0.0)
            running_sum = running_sum * jnp.exp(running_max - new_max) + jnp.sum(weights, axis=-1)
            return (new_max, running_sum)

        start_state = (
            jnp.full((heads_here, block_width), masked_low, jnp.float32),
            jnp.zeros((heads_here, block_width), jnp.float32),
        )
        running_max, running_sum = lax.fori_loop(0, i + 1, stats_inner, start_state)
        return lax.dynamic_update_slice_in_dim(
            log_totals, running_max + jnp.log(running_sum), i * block_width, 1
        )

    log_totals = lax.fori_loop(
        0, block_count, stats_row, jnp.zeros((heads_here, length), jnp.float32)
    )

    def out_row(i, out_all):
        query_block = take_block(query_part, i, block_width)
        log_block = lax.dynamic_slice_in_dim(log_totals, i * block_width, block_width, 1)

        def out_inner(j, accum_out):
            scores = block_scores(query_block, take_block(key_part, j, block_width), inv_root)
            allowed = block_mask(seg_all, i * block_width, j * block_width, block_width)[None]
            probs_low = jnp.where(allowed, jnp.exp(scores - log_block[..., None]), 0.0).astype(
                jnp.bfloat16
            )
            return accum_out + jnp.einsum(
                "hqk,khd->qhd",
                probs_low,
                take_block(value_part, j, block_width),
                preferred_element_type=jnp.float32,
            )

        accum_out = lax.fori_loop(
            0, i + 1, out_inner, jnp.zeros((block_width, heads_here, head_size), jnp.float32)
        )
        return lax.dynamic_update_slice_in_dim(
            out_all, accum_out.astype(jnp.bfloat16), i * block_width, 0
        )

    out_all = lax.fori_loop(
        0, block_count, out_row, jnp.zeros((length, heads_here, head_size), jnp.bfloat16)
    )
    return (out_all, log_totals)


def attend_grads(query_part, key_part, value_part, seg_all, out_part, log_totals, grad_part):
    length, heads_here, head_size = query_part.shape
    block_width = min(512, length)
    block_count = length // block_width
    inv_root = 1.0 / math.sqrt(head_size)
    row_dots = jnp.einsum("qhd,qhd->hq", grad_part, out_part, preferred_element_type=jnp.float32)

    def grad_row(i, state_now):
        query_all, key_all, value_all = state_now
        query_block = take_block(query_part, i, block_width)
        grad_block = take_block(grad_part, i, block_width)
        log_block = lax.dynamic_slice_in_dim(log_totals, i * block_width, block_width, 1)
        dots_block = lax.dynamic_slice_in_dim(row_dots, i * block_width, block_width, 1)

        def grad_inner(j, inner_state):
            query_accum, key_accum, value_accum = inner_state
            key_block = take_block(key_part, j, block_width)
            value_block = take_block(value_part, j, block_width)
            scores = block_scores(query_block, key_block, inv_root)
            allowed = block_mask(seg_all, i * block_width, j * block_width, block_width)[None]
            probs = jnp.where(allowed, jnp.exp(scores - log_block[..., None]), 0.0)
            probs_low = probs.astype(jnp.bfloat16)
            value_new = take_block(value_accum, j, block_width) + jnp.einsum(
                "hqk,qhd->khd", probs_low, grad_block, preferred_element_type=jnp.float32
            )
            value_accum = lax.dynamic_update_slice_in_dim(
                value_accum, value_new, j * block_width, 0
            )
            prob_grad = jnp.einsum(
                "qhd,khd->hqk", grad_block, value_block, preferred_element_type=jnp.float32
            )
            score_grad = (probs * (prob_grad - dots_block[..., None])).astype(jnp.bfloat16)
            query_accum = query_accum + jnp.einsum(
                "hqk,khd->qhd", score_grad, key_block, preferred_element_type=jnp.float32
            )
            key_new = take_block(key_accum, j, block_width) + jnp.einsum(
                "hqk,qhd->khd", score_grad, query_block, preferred_element_type=jnp.float32
            )
            key_accum = lax.dynamic_update_slice_in_dim(key_accum, key_new, j * block_width, 0)
            return (query_accum, key_accum, value_accum)

        start_state = (
            jnp.zeros((block_width, heads_here, head_size), jnp.float32),
            key_all,
            value_all,
        )
        query_accum, key_all, value_all = lax.fori_loop(0, i + 1, grad_inner, start_state)
        query_all = lax.dynamic_update_slice_in_dim(
            query_all, (query_accum * inv_root).astype(jnp.bfloat16), i * block_width, 0
        )
        return (query_all, key_all, value_all)

    zero_grads = jnp.zeros((length, heads_here, head_size), jnp.float32)
    start_all = (jnp.zeros((length, heads_here, head_size), jnp.bfloat16), zero_grads, zero_grads)
    query_all, key_all, value_all = lax.fori_loop(0, block_count, grad_row, start_all)
    return (query_all, (key_all * inv_root).astype(jnp.bfloat16), value_all.astype(jnp.bfloat16))


def body(activations, queries, key_weight, value_weight, segment_ids, out_grad):
    rows_here = activations.shape[1]
    inputs = activations[0]
    kv_width = key_weight.shape[1]
    seq_devices = lax.axis_size("seq")
    heads_here = HEADS // seq_devices
    kv_group = HEADS // KV_HEADS
    stacked = jnp.concatenate([key_weight, value_weight], axis=1)
    columns = inputs
    projected = jnp.dot(
        columns,
        lax.all_gather(stacked, ("seq", "fsdp"), axis=0, tiled=True),
        preferred_element_type=jnp.float32,
    )
    projected = projected.astype(jnp.bfloat16)
    key_rows = projected[:, :kv_width].reshape(rows_here, KV_HEADS, HEAD_DIM)
    value_rows = projected[:, kv_width:].reshape(rows_here, KV_HEADS, HEAD_DIM)
    kv_copies = max(kv_group // heads_here, 1)
    query_heads = queries[0].reshape(rows_here, HEADS, HEAD_DIM)
    sent = (
        query_heads,
        jnp.repeat(key_rows, kv_copies, axis=1),
        jnp.repeat(value_rows, kv_copies, axis=1),
    )
    query_part, key_part, value_part = (
        lax.all_to_all(sent[0], "seq", split_axis=1, concat_axis=0, tiled=True),
        lax.all_to_all(sent[1], "seq", split_axis=1, concat_axis=0, tiled=True),
        lax.all_to_all(sent[2], "seq", split_axis=1, concat_axis=0, tiled=True),
    )
    widen_by = heads_here // key_part.shape[1]
    key_part = jnp.repeat(key_part, widen_by, axis=1)
    value_part = jnp.repeat(value_part, widen_by, axis=1)
    seg_all = lax.all_gather(segment_ids[0], "seq", axis=0, tiled=True)
    out_part, log_totals = attend(query_part, key_part, value_part, seg_all)
    context = lax.all_to_all(out_part, "seq", split_axis=0, concat_axis=1, tiled=True).reshape(
        1, rows_here, HEADS * HEAD_DIM
    )
    grad_part = lax.all_to_all(
        out_grad[0].reshape(rows_here, HEADS, HEAD_DIM),
        "seq",
        split_axis=1,
        concat_axis=0,
        tiled=True,
    )
    query_back, key_back, value_back = attend_grads(
        query_part, key_part, value_part, seg_all, out_part, log_totals, grad_part
    )
    query_tok, key_tok, value_tok = (
        lax.all_to_all(query_back, "seq", split_axis=0, concat_axis=1, tiled=True),
        lax.all_to_all(key_back, "seq", split_axis=0, concat_axis=1, tiled=True),
        lax.all_to_all(value_back, "seq", split_axis=0, concat_axis=1, tiled=True),
    )
    key_sum = (
        key_tok.reshape(rows_here, KV_HEADS, kv_group, HEAD_DIM).astype(jnp.float32).sum(axis=2)
    )
    value_sum = (
        value_tok.reshape(rows_here, KV_HEADS, kv_group, HEAD_DIM).astype(jnp.float32).sum(axis=2)
    )
    grad_kv = jnp.concatenate(
        [
            key_sum.astype(jnp.bfloat16).reshape(rows_here, kv_width),
            value_sum.astype(jnp.bfloat16).reshape(rows_here, kv_width),
        ],
        axis=1,
    )
    input_grad = lax.dot_general(
        grad_kv,
        lax.all_gather(stacked, ("seq", "fsdp"), axis=0, tiled=True),
        (((1,), (1,)), ((), ())),
        preferred_element_type=jnp.float32,
    )
    input_grad = input_grad.astype(jnp.bfloat16).reshape(1, rows_here, inputs.shape[1])
    columns = inputs
    grad_shard = lax.psum_scatter(
        lax.dot_general(
            columns, grad_kv, (((0,), (0,)), ((), ())), preferred_element_type=jnp.float32
        ).astype(jnp.bfloat16),
        ("seq", "fsdp"),
        scatter_dimension=0,
        tiled=True,
    ).astype(jnp.float32)
    grad_total = lax.psum(grad_shard, "rep").astype(jnp.bfloat16)
    query_grad = query_tok.reshape(1, rows_here, HEADS * HEAD_DIM)
    return (context, query_grad, input_grad, grad_total[:, :kv_width], grad_total[:, kv_width:])


def solution(mesh):
    return jax.shard_map(
        body,
        mesh=mesh,
        in_specs=(
            P(("groups", "rep", "fsdp"), "seq", None),
            P(("groups", "rep", "fsdp"), "seq", None),
            P(("seq", "fsdp"), None),
            P(("seq", "fsdp"), None),
            P(("groups", "rep", "fsdp"), "seq"),
            P(("groups", "rep", "fsdp"), "seq", None),
        ),
        out_specs=(
            P(("groups", "rep", "fsdp"), "seq", None),
            P(("groups", "rep", "fsdp"), "seq", None),
            P(("groups", "rep", "fsdp"), "seq", None),
            P(("groups", "seq", "fsdp"), None),
            P(("groups", "seq", "fsdp"), None),
        ),
        check_vma=False,
    )
```

profile of v0, /device:TPU:0, one launch (start us, length us, event | category | flops | bytes accessed | tf_op | source)
XLA Modules:
  0.0 248.5 jit_solution(1533762481953320926)
XLA Ops:
  7.2 1.9 pad_maximum_fusion
  9.2 2.0 copy.45
  11.2 6.3 %all-to-all-start.1 = ((bf16[128,16,128]{0,2,1:T(8,128)(2,1)}), bf16[128,16,128]{0,2,1:T(8,128)(2,1)S(1)}, u32[]{:S(2)}, u32[]{:S(2)}) async-start(bf16[128,16,128]{0,2,1:T(8,128)(2,1)} %bitcast.9), calls=%async_computation.1 | async-start | bytes 1048576 | tf_op jit(solution)/shard_map/all_to_all | solution.py:177
  17.5 2.0 copy.52
  19.6 24.7 %all-to-all-done.1 = bf16[128,16,128]{0,2,1:T(8,128)(2,1)S(1)} async-done(((bf16[128,16,128]{0,2,1:T(8,128)(2,1)}), bf16[128,16,128]{0,2,1:T(8,128)(2,1)S(1)}, u32[]{:S(2)}, u32[]{:S(2)}) %all-to-all-start.1) | async-done | bytes 524320 | tf_op jit(solution)/shard_map/all_to_all | solution.py:177
  44.2 3.6 %all-to-all-start.4 = ((bf16[128,16,128]{0,2,1:T(8,128)(2,1)}), bf16[128,16,128]{0,2,1:T(8,128)(2,1)S(1)}, u32[]{:S(2)}, u32[]{:S(2)}) async-start(bf16[128,16,128]{0,2,1:T(8,128)(2,1)} %bitcast.22), calls=%async_computation.4 | async-start | bytes 1048576 | tf_op jit(solution)/shard_map/all_to_all | solution.py:189
  47.9 21.7 %all-gather = s32[1,512]{1,0:T(1,128)S(1)} all-gather(s32[1,128]{1,0:T(1,128)S(1)} %copy-done.3), channel_id=2, replica_groups=mesh['groups'=2,'seq'=4,'rep'=2,'fsdp'=2] {'seq'}, dimensions={1}, use_global_device_ids=true | all-gather | bytes 2560 | tf_op jit(solution)/shard_map/all_gather | solution.py:184
  69.5 9.1 %all-gather.3.cloned.1.call-done = bf16[2048,1024]{1,0:T(8,128)(2,1)} async-done(((bf16[256,1024]{1,0:T(8,128)(2,1)}), bf16[2048,1024]{1,0:T(8,128)(2,1)}) %all-gather.3.cloned.1.call-update) | async-done | bytes 4194320 | tf_op jit(solution)/shard_map/all_gather | solution.py:163
  78.7 3.5 %fusion.11 = bf16[128,1024]{0,1:T(8,128)(2,1)S(1)} fusion(bf16[2048,1024]{1,0:T(8,128)(2,1)} %all-gather.3.cloned.1.call-done, bf16[1,128,2048]{2,1,0:T(8,128)(2,1)S(1)} %copy-done), kind=kOutput, calls=%fused_computation.22 | convolution fusion | flops 537001984 | bytes 4980736 | tf_op jit(solution)/shard_map/dot_general | solution.py:161
  82.2 0.8 copy.44
  83.0 3.3 %all-to-all-start = ((bf16[128,4,128]{2,0,1:T(8,128)(2,1)}), bf16[128,4,128]{2,0,1:T(8,128)(2,1)S(1)}, u32[]{:S(2)}, u32[]{:S(2)}) async-start(bf16[128,4,128]{2,0,1:T(8,128)(2,1)} %copy.44), calls=%async_computation | async-start | bytes 262144 | tf_op jit(solution)/shard_map/all_to_all | solution.py:178
  86.5 0.3 copy.47
  86.8 0.3 copy.54
  87.1 0.8 copy.48
  87.9 4.8 %all-to-all-done = bf16[128,4,128]{2,0,1:T(8,128)(2,1)S(1)} async-done(((bf16[128,4,128]{2,0,1:T(8,128)(2,1)}), bf16[128,4,128]{2,0,1:T(8,128)(2,1)S(1)}, u32[]{:S(2)}, u32[]{:S(2)}) %all-to-all-start) | async-done | bytes 131104 | tf_op jit(solution)/shard_map/all_to_all | solution.py:178
  92.7 3.3 %all-to-all-start.2 = ((bf16[128,4,128]{2,0,1:T(8,128)(2,1)}), bf16[128,4,128]{2,0,1:T(8,128)(2,1)S(1)}, u32[]{:S(2)}, u32[]{:S(2)}) async-start(bf16[128,4,128]{2,0,1:T(8,128)(2,1)} %copy.48), calls=%async_computation.2 | async-start | bytes 262144 | tf_op jit(solution)/shard_map/all_to_all | solution.py:179
  96.0 0.9 fusion.3
  96.9 1.0 select_reduce_fusion
  98.0 0.9 fusion.10
  99.0 1.2 copy.60
  100.2 1.8 all-to-all-done.2
  101.9 3.5 %all-to-all-start.7 = ((bf16[512,4,128]{2,1,0:T(4,128)(2,1)}), bf16[512,4,128]{2,1,0:T(4,128)(2,1)S(1)}, u32[]{:S(2)}, u32[]{:S(2)}) async-start(bf16[512,4,128]{2,1,0:T(4,128)(2,1)} %copy.60), calls=%async_computation.7 | async-start | bytes 1048576 | tf_op jit(solution)/shard_map/all_to_all | solution.py:202
  105.4 3.9 %fusion.12 = (f32[4,512]{1,0:T(4,128)S(1)}, bf16[4,512,128]{2,1,0:T(8,128)(2,1)S(1)}) fusion(bf16[4,128,4,128]{3,1,0,2:T(8,128)(2,1)S(1)} %copy.54, bf16[512,128]{1,0:T(8,128)(2,1)S(1)} %bitcast.111, f32[4,512,512]{2,1,0:T(8,128)} %copy-done.1, f32[4,512]{1,0:T(4,128)S(1)} %log_add_fusion, pred[512,512]{0,1:T(8,128)(4,1)S(1)} %fusion.13), kind=kOutput, calls=%fused_computation.24 | convolution fusion | flops 273938432 | bytes 5652480 | tf_op jit(solution)/shard_map/while/body/eval_jaxpr/while/body/hqk,khd->qhd/dot_general | solution.py:74
  109.3 1.4 fusion
  110.8 0.7 fusion.8
  111.5 0.6 copy-done.4
  112.1 1.2 copy.58
  113.3 5.2 %all-to-all-done.7 = bf16[512,4,128]{2,1,0:T(4,128)(2,1)S(1)} async-done(((bf16[512,4,128]{2,1,0:T(4,128)(2,1)}), bf16[512,4,128]{2,1,0:T(4,128)(2,1)S(1)}, u32[]{:S(2)}, u32[]{:S(2)}) %all-to-all-start.7) | async-done | bytes 524320 | tf_op jit(solution)/shard_map/all_to_all | solution.py:202
  118.5 3.5 %all-to-all-start.6 = ((bf16[512,4,128]{2,1,0:T(4,128)(2,1)}), bf16[512,4,128]{2,1,0:T(4,128)(2,1)S(1)}, u32[]{:S(2)}, u32[]{:S(2)}) async-start(bf16[512,4,128]{2,1,0:T(4,128)(2,1)} %copy.58), calls=%async_computation.6 | async-start | bytes 1048576 | tf_op jit(solution)/shard_map/all_to_all | solution.py:201
  122.0 0.2 reduce-scatter.2.cloned.1.call-start
  122.2 0.7 reduce_sum.48
  123.0 12.3 %all-to-all-done.6 = bf16[512,4,128]{2,1,0:T(4,128)(2,1)S(1)} async-done(((bf16[512,4,128]{2,1,0:T(4,128)(2,1)}), bf16[512,4,128]{2,1,0:T(4,128)(2,1)S(1)}, u32[]{:S(2)}, u32[]{:S(2)}) %all-to-all-start.6) | async-done | bytes 524320 | tf_op jit(solution)/shard_map/all_to_all | solution.py:201
  135.3 0.7 reduce_sum.45
  136.1 3.2 %convert_bitcast_fusion = bf16[2048,1024]{0,1:T(8,128)(2,1)} fusion(bf16[1,128,2048]{2,1,0:T(8,128)(2,1)S(1)} %copy-done, bf16[128,512]{0,1:T(8,128)(2,1)S(1)} %bitcast.98, bf16[128,512]{0,1:T(8,128)(2,1)S(1)} %bitcast.100), kind=kOutput, calls=%fused_computation.6 | convolution fusion | flops 539492352 | bytes 4980736 | tf_op jit(solution)/shard_map/dot_general | solution.py:226
  139.4 1.2 copy.50
  140.6 3.5 %all-to-all-start.3 = ((bf16[512,4,128]{2,1,0:T(4,128)(2,1)}), bf16[512,4,128]{2,1,0:T(4,128)(2,1)S(1)}, u32[]{:S(2)}, u32[]{:S(2)}) async-start(bf16[512,4,128]{2,1,0:T(4,128)(2,1)} %copy.50), calls=%async_computation.3 | async-start | bytes 1048576 | tf_op jit(solution)/shard_map/all_to_all | solution.py:186
  144.1 0.9 fusion.9
  145.0 1.2 copy.56
  146.2 19.1 %all-to-all-done.3 = bf16[512,4,128]{2,1,0:T(4,128)(2,1)S(1)} async-done(((bf16[512,4,128]{2,1,0:T(4,128)(2,1)}), bf16[512,4,128]{2,1,0:T(4,128)(2,1)S(1)}, u32[]{:S(2)}, u32[]{:S(2)}) %all-to-all-start.3) | async-done | bytes 524320 | tf_op jit(solution)/shard_map/all_to_all | solution.py:186
  165.3 4.3 %all-to-all-start.5 = ((bf16[512,4,128]{2,1,0:T(4,128)(2,1)}), bf16[512,4,128]{2,1,0:T(4,128)(2,1)S(1)}, u32[]{:S(2)}, u32[]{:S(2)}) async-start(bf16[512,4,128]{2,1,0:T(4,128)(2,1)} %copy.56), calls=%async_computation.5 | async-start | bytes 1048576 | tf_op jit(solution)/shard_map/all_to_all | solution.py:200
  169.6 34.6 %reduce-scatter.2.cloned.1.call-done = bf16[256,1024]{0,1:T(8,128)(2,1)} async-done(((bf16[2048,1024]{0,1:T(8,128)(2,1)}), bf16[256,1024]{0,1:T(8,128)(2,1)}) %reduce-scatter.2.cloned.1.call-update) | async-done | bytes 524304 | tf_op jit(solution)/shard_map/reduce_scatter | solution.py:225
  204.4 1.2 reshape.232
  205.8 1.2 reshape.233
  207.0 4.5 %fusion.5 = bf16[1,128,2048]{2,1,0:T(8,128)(2,1)} fusion(bf16[2048,1024]{1,0:T(8,128)(2,1)} %all-gather.3.cloned.1.call-done, bf16[128,512]{0,1:T(8,128)(2,1)S(1)} %bitcast.99, bf16[128,512]{0,1:T(8,128)(2,1)S(1)} %bitcast.101), kind=kOutput, calls=%fused_computation.11 | convolution fusion | flops 537657344 | bytes 4980736 | tf_op jit(solution)/shard_map/dot_general | solution.py:217
  211.5 27.7 %all-reduce.2.cloned.1.call-done = bf16[256,1024]{0,1:T(8,128)(2,1)} async-done(((bf16[256,1024]{0,1:T(8,128)(2,1)}), bf16[256,1024]{0,1:T(8,128)(2,1)}) %all-reduce.2.cloned.1.call-update) | async-done | bytes 524304 | tf_op jit(solution)/shard_map/psum | solution.py:233
  239.2 1.1 fusion.25
  240.2 0.8 copy.63
  241.1 0.8 copy.62
  (26 shorter events, 1.0 us)
Async XLA Ops:
  7.2 71.5 %copy-start = (bf16[1,128,2048]{2,1,0:T(8,128)(2,1)S(1)}, bf16[1,128,2048]{2,1,0:T(8,128)(2,1)}, u32[]{:S(2)}) copy-start(bf16[1,128,2048]{2,1,0:T(8,128)(2,1)} %param.6) | copy-start | bytes 1572868
  7.2 40.7 %copy-start.3 = (s32[1,128]{1,0:T(1,128)S(1)}, s32[1,128]{1,0:T(1,128)}, u32[]{:S(2)}) copy-start(s32[1,128]{1,0:T(1,128)} %param.10) | copy-start | bytes 1540
  7.2 71.5 %all-gather.3.cloned.1.call-start = ((), (), s32[]{:S(2)}) async-start(), calls=%async_computation.9 | async-start | bytes 4718592 | tf_op jit(solution)/shard_map/all_gather | solution.py:163
  11.2 33.0 %all-to-all-start.1 = ((bf16[128,16,128]{0,2,1:T(8,128)(2,1)}), bf16[128,16,128]{0,2,1:T(8,128)(2,1)S(1)}, u32[]{:S(2)}, u32[]{:S(2)}) async-start(bf16[128,16,128]{0,2,1:T(8,128)(2,1)} %bitcast.9), calls=%async_computation.1 | async-start | bytes 1048576 | tf_op jit(solution)/shard_map/all_to_all | solution.py:177
  44.2 38.7 %all-to-all-start.4 = ((bf16[128,16,128]{0,2,1:T(8,128)(2,1)}), bf16[128,16,128]{0,2,1:T(8,128)(2,1)S(1)}, u32[]{:S(2)}, u32[]{:S(2)}) async-start(bf16[128,16,128]{0,2,1:T(8,128)(2,1)} %bitcast.22), calls=%async_computation.4 | async-start | bytes 1048576 | tf_op jit(solution)/shard_map/all_to_all | solution.py:189
  83.0 9.7 %all-to-all-start = ((bf16[128,4,128]{2,0,1:T(8,128)(2,1)}), bf16[128,4,128]{2,0,1:T(8,128)(2,1)S(1)}, u32[]{:S(2)}, u32[]{:S(2)}) async-start(bf16[128,4,128]{2,0,1:T(8,128)(2,1)} %copy.44), calls=%async_computation | async-start | bytes 262144 | tf_op jit(solution)/shard_map/all_to_all | solution.py:178
  92.7 9.2 %all-to-all-start.2 = ((bf16[128,4,128]{2,0,1:T(8,128)(2,1)}), bf16[128,4,128]{2,0,1:T(8,128)(2,1)S(1)}, u32[]{:S(2)}, u32[]{:S(2)}) async-start(bf16[128,4,128]{2,0,1:T(8,128)(2,1)} %copy.48), calls=%async_computation.2 | async-start | bytes 262144 | tf_op jit(solution)/shard_map/all_to_all | solution.py:179
  96.9 2.0 copy-start.1
  101.9 16.6 %all-to-all-start.7 = ((bf16[512,4,128]{2,1,0:T(4,128)(2,1)}), bf16[512,4,128]{2,1,0:T(4,128)(2,1)S(1)}, u32[]{:S(2)}, u32[]{:S(2)}) async-start(bf16[512,4,128]{2,1,0:T(4,128)(2,1)} %copy.60), calls=%async_computation.7 | async-start | bytes 1048576 | tf_op jit(solution)/shard_map/all_to_all | solution.py:202
  105.4 3.9 %copy-start.2 = (f32[4,512,512]{2,1,0:T(8,128)S(1)}, f32[4,512,512]{2,1,0:T(8,128)}, u32[]{:S(2)}) copy-start(f32[4,512,512]{2,1,0:T(8,128)} %copy-done.1) | copy-start | bytes 12582916
  110.7 1.4 copy-start.4
  118.5 16.8 %all-to-all-start.6 = ((bf16[512,4,128]{2,1,0:T(4,128)(2,1)}), bf16[512,4,128]{2,1,0:T(4,128)(2,1)S(1)}, u32[]{:S(2)}, u32[]{:S(2)}) async-start(bf16[512,4,128]{2,1,0:T(4,128)(2,1)} %copy.58), calls=%async_computation.6 | async-start | bytes 1048576 | tf_op jit(solution)/shard_map/all_to_all | solution.py:201
  122.0 82.2 %reduce-scatter.2.cloned.1.call-start = ((), (), s32[]{:S(2)}) async-start(), calls=%async_computation.10 | async-start | bytes 4718592 | tf_op jit(solution)/shard_map/reduce_scatter | solution.py:225
  139.3 4.7 %copy-start.5 = (bf16[4,512,512]{1,2,0:T(8,128)(2,1)S(1)}, bf16[4,512,512]{1,2,0:T(8,128)(2,1)}, u32[]{:S(2)}) copy-start(bf16[4,512,512]{1,2,0:T(8,128)(2,1)} %copy-done.4) | copy-start | bytes 6291460
  140.6 24.7 %all-to-all-start.3 = ((bf16[512,4,128]{2,1,0:T(4,128)(2,1)}), bf16[512,4,128]{2,1,0:T(4,128)(2,1)S(1)}, u32[]{:S(2)}, u32[]{:S(2)}) async-start(bf16[512,4,128]{2,1,0:T(4,128)(2,1)} %copy.50), calls=%async_computation.3 | async-start | bytes 1048576 | tf_op jit(solution)/shard_map/all_to_all | solution.py:186
  165.3 40.3 %all-to-all-start.5 = ((bf16[512,4,128]{2,1,0:T(4,128)(2,1)}), bf16[512,4,128]{2,1,0:T(4,128)(2,1)S(1)}, u32[]{:S(2)}, u32[]{:S(2)}) async-start(bf16[512,4,128]{2,1,0:T(4,128)(2,1)} %copy.56), calls=%async_computation.5 | async-start | bytes 1048576 | tf_op jit(solution)/shard_map/all_to_all | solution.py:200
  169.6 69.6 %all-reduce.2.cloned.1.call-start = ((), (), s32[]{:S(2)}) async-start(), calls=%async_computation.11 | async-start | bytes 1048576 | tf_op jit(solution)/shard_map/psum | solution.py:233
Sparse Core Ops, SparseCore 0:
  10.2 68.4 all-gather.2
  139.5 64.6 reduce-scatter.1
  206.5 32.6 all-reduce.1
where the time goes:
time: 249 us; the launch traced here: 248 us
  waiting for transfers between devices  139 us (56%)
  starting transfers between devices  31.6 us (13%)
  blocking collectives  21.7 us (9%)
  matrix products  19.9 us (8%)
  local copies, waits for them, and re-layouts  17.4 us (7%)
  between operations  14 us (6%)
  other arithmetic  4.52 us (2%)
    reduce_scatter x1, waiting for transfers between devices, body(): lax.psum_scatter(lax.dot_general(columns, grad_kv, (((0,), (0,)), ((), ()...  34.6 us
    psum x1, waiting for transfers between devices, body(): grad_total = lax.psum(grad_shard, 'rep').astype(jnp.bfloat16)  27.7 us
    all_to_all x1, waiting for transfers between devices, body(): lax.all_to_all(sent[0], 'seq', split_axis=1, concat_axis=0, tiled=True)  24.7 us
    all_gather x1, blocking collectives, body(): seg_all = lax.all_gather(segment_ids[0], 'seq', axis=0, tiled=True)  21.7 us
    all_to_all x1, waiting for transfers between devices, body(): lax.all_to_all(out_part, 'seq', split_axis=0, concat_axis=1, tiled=True)  19.1 us
    all_to_all x1, waiting for transfers between devices, body(): lax.all_to_all(key_back, 'seq', split_axis=0, concat_axis=1, tiled=True)  12.3 us
    all_gather x1, waiting for transfers between devices, body(): lax.all_gather(stacked, ('seq', 'fsdp'), axis=0, tiled=True)  9.14 us
    unnamed x16, local copies, waits for them, and re-layouts  6.44 us
  transfers between devices with their start and end apart: 11, of which 9 were waited for; matrix products, arithmetic and copies ran while one was open for 13% of the time, Pallas kernels for 0%

commit v1 on v0

--- a/solution.py
+++ b/solution.py
@@ -8,6 +8,34 @@
 KV_HEADS = 4
 HEAD_DIM = 128
 masked_low = -1e30
+
+
+def cover_group_for(payload, dim_no, matrix):
+    plain, prior = (payload.shape[:dim_no], payload.shape[dim_no + 1 :])
+    e_next = payload.reshape(*plain, matrix, -1, *prior)
+    return jnp.moveaxis(e_next, dim_no, 0)
+
+
+def part_links(local_values, dim_i):
+    b_now = list(local_values.shape[1:])
+    b_now[dim_i] *= local_values.shape[0]
+    return jnp.moveaxis(local_values, 0, dim_i).reshape(b_now)
+
+
+def _rest_wires(group_axis, sample, view, page):
+    v1 = lax.axis_index(group_axis)
+    tile_out = lax.axis_size(group_axis)
+    kept_arr, left_arr = (tile_out, v1)
+    step_out = cover_group_for(page, view, kept_arr)
+    formed = step_out
+    for idx in range(1, kept_arr):
+        n_now, met_up = ((left_arr + idx) % kept_arr, (left_arr - idx) % kept_arr)
+        current_arr = lax.dynamic_index_in_dim(step_out, n_now, 0)
+        m_next = lax.ppermute(
+            current_arr, group_axis, [(dev, (dev + idx) % kept_arr) for dev in range(kept_arr)]
+        )
+        formed = lax.dynamic_update_slice_in_dim(formed, m_next, met_up, axis=0)
+    return part_links(formed, sample)
 
 
 def block_mask(seg_all, row_start, col_start, block_width):
@@ -174,7 +202,7 @@
         jnp.repeat(value_rows, kv_copies, axis=1),
     )
     query_part, key_part, value_part = (
-        lax.all_to_all(sent[0], "seq", split_axis=1, concat_axis=0, tiled=True),
+        _rest_wires("seq", sample=0, view=1, page=sent[0]),
         lax.all_to_all(sent[1], "seq", split_axis=1, concat_axis=0, tiled=True),
         lax.all_to_all(sent[2], "seq", split_axis=1, concat_axis=0, tiled=True),
     )

time: 249 us -> 245 us (0.984)
  waiting for transfers between devices: 139 us -> 126 us
  blocking collectives: 21.7 us -> 28.2 us
    all_to_all x1 -> x0, waiting for transfers between devices: 24.7 us -> none  [body(): lax.all_to_all(sent[0], 'seq', split_axis=1, concat_axis=0, tiled=True)]
    all_gather x1, waiting for transfers between devices: 9.14 us -> 22.2 us  [body(): lax.all_gather(stacked, ('seq', 'fsdp'), axis=0, tiled=True)]
    all_gather x1, blocking collectives: 21.7 us -> 28.2 us  [body(): seg_all = lax.all_gather(segment_ids[0], 'seq', axis=0, tiled=True)]
    all_to_all x1 -> x0, starting transfers between devices: 6.32 us -> none  [body(): lax.all_to_all(sent[0], 'seq', split_axis=1, concat_axis=0, tiled=True)]
    ppermute x0 -> x3, starting transfers between devices: none -> 6.11 us  [_rest_wires(): lax.ppermute(current_arr, group_axis, [(dev, (dev + idx) % kept_arr) for...]
    unnamed x16 -> x13, local copies, waits for them, and re-layouts: 6.44 us -> 4.39 us
  transfers between devices with their start and end apart: 11 -> 13, of which waited for: 9 -> 8; matrix products, arithmetic and copies ran while one was open for 13% -> 14% of each run, Pallas kernels for 0% -> 0%
where the time goes in v1:
time: 245 us; the launch traced here: 244 us
  waiting for transfers between devices  126 us (51%)
  starting transfers between devices  32.8 us (13%)
  blocking collectives  28.2 us (12%)
  matrix products  21.7 us (9%)
  local copies, waits for them, and re-layouts  17.1 us (7%)
  between operations  14.1 us (6%)
  other arithmetic  4.52 us (2%)
    reduce_scatter x1, waiting for transfers between devices, body(): lax.psum_scatter(lax.dot_general(columns, grad_kv, (((0,), (0,)), ((), ()...  34.9 us
    all_gather x1, blocking collectives, body(): seg_all = lax.all_gather(segment_ids[0], 'seq', axis=0, tiled=True)  28.2 us
    psum x1, waiting for transfers between devices, body(): grad_total = lax.psum(grad_shard, 'rep').astype(jnp.bfloat16)  28 us
    all_gather x1, waiting for transfers between devices, body(): lax.all_gather(stacked, ('seq', 'fsdp'), axis=0, tiled=True)  22.2 us
    all_to_all x1, waiting for transfers between devices, body(): lax.all_to_all(out_part, 'seq', split_axis=0, concat_axis=1, tiled=True)  16.9 us
    all_to_all x1, waiting for transfers between devices, body(): lax.all_to_all(key_back, 'seq', split_axis=0, concat_axis=1, tiled=True)  12.1 us
    ppermute x3, starting transfers between devices, _rest_wires(): lax.ppermute(current_arr, group_axis, [(dev, (dev + idx) % kept_arr) for...  6.11 us
    all_to_all x1, waiting for transfers between devices, body(): lax.all_to_all(value_back, 'seq', split_axis=0, concat_axis=1, tiled=True)  5.02 us
  transfers between devices with their start and end apart: 13, of which 8 were waited for; matrix products, arithmetic and copies ran while one was open for 14% of the time, Pallas kernels for 0%

profile of v1, /device:TPU:0, one launch (start us, length us, event | category | flops | bytes accessed | tf_op | source)
XLA Modules:
  0.0 244.3 jit_solution(13120320076566524262)
XLA Ops:
  7.2 1.9 pad_maximum_fusion
  9.2 1.4 reshape_reshape_squeeze.3
  10.8 5.1 %collective-permute-start.2 = (bf16[1,128,4,128]{3,2,0,1:T(4,128)(2,1)S(1)}, bf16[1,128,4,128]{3,2,0,1:T(4,128)(2,1)S(1)}, u32[]{:S(2)}, u32[]{:S(2)}) collective-permute-start(bf16[1,128,4,128]{3,2,0,1:T(4,128)(2,1)S(1)} %get-tuple-element.282), channel_id=1, source_target_pairs={{0,12},{4,0},{8,4},{12,8},{1,13},{5,1},{9,5},{13,9},{2,14},{6,2},{... | collective-permute-start | bytes 393224 | tf_op jit(solution)/shard_map/ppermute | solution.py:34
  15.9 1.0 collective-permute-start
  16.9 2.0 copy.49
  19.0 4.1 %all-to-all-start.3 = ((bf16[128,16,128]{0,2,1:T(8,128)(2,1)}), bf16[128,16,128]{0,2,1:T(8,128)(2,1)S(1)}, u32[]{:S(2)}, u32[]{:S(2)}) async-start(bf16[128,16,128]{0,2,1:T(8,128)(2,1)} %bitcast.21), calls=%async_computation.3 | async-start | bytes 1048576 | tf_op jit(solution)/shard_map/all_to_all | solution.py:217
  23.1 28.2 %all-gather = s32[1,512]{1,0:T(1,128)S(1)} all-gather(s32[1,128]{1,0:T(1,128)S(1)} %copy-done.3), channel_id=2, replica_groups=mesh['groups'=2,'seq'=4,'rep'=2,'fsdp'=2] {'seq'}, dimensions={1}, use_global_device_ids=true | all-gather | bytes 2560 | tf_op jit(solution)/shard_map/all_gather | solution.py:212
  51.2 0.2 fusion.10
  51.6 22.2 %all-gather.3.cloned.1.call-done = bf16[2048,1024]{1,0:T(8,128)(2,1)} async-done(((bf16[256,1024]{1,0:T(8,128)(2,1)}), bf16[2048,1024]{1,0:T(8,128)(2,1)}) %all-gather.3.cloned.1.call-update) | async-done | bytes 4194320 | tf_op jit(solution)/shard_map/all_gather | solution.py:191
  73.8 3.5 %fusion.8 = bf16[128,1024]{0,1:T(8,128)(2,1)S(1)} fusion(bf16[2048,1024]{1,0:T(8,128)(2,1)} %all-gather.3.cloned.1.call-done, bf16[1,128,2048]{2,1,0:T(8,128)(2,1)S(1)} %copy-done), kind=kOutput, calls=%fused_computation.19 | convolution fusion | flops 537001984 | bytes 4980736 | tf_op jit(solution)/shard_map/dot_general | solution.py:189
  77.4 0.8 copy.44
  78.1 4.7 %all-to-all-start = ((bf16[128,4,128]{2,0,1:T(8,128)(2,1)}), bf16[128,4,128]{2,0,1:T(8,128)(2,1)S(1)}, u32[]{:S(2)}, u32[]{:S(2)}) async-start(bf16[128,4,128]{2,0,1:T(8,128)(2,1)} %copy.44), calls=%async_computation | async-start | bytes 262144 | tf_op jit(solution)/shard_map/all_to_all | solution.py:206
  83.2 0.3 copy.51
  83.4 0.8 copy.45
  84.2 4.9 %all-to-all-done = bf16[128,4,128]{2,0,1:T(8,128)(2,1)S(1)} async-done(((bf16[128,4,128]{2,0,1:T(8,128)(2,1)}), bf16[128,4,128]{2,0,1:T(8,128)(2,1)S(1)}, u32[]{:S(2)}, u32[]{:S(2)}) %all-to-all-start) | async-done | bytes 131104 | tf_op jit(solution)/shard_map/all_to_all | solution.py:206
  89.1 3.3 %all-to-all-start.1 = ((bf16[128,4,128]{2,0,1:T(8,128)(2,1)}), bf16[128,4,128]{2,0,1:T(8,128)(2,1)S(1)}, u32[]{:S(2)}, u32[]{:S(2)}) async-start(bf16[128,4,128]{2,0,1:T(8,128)(2,1)} %copy.45), calls=%async_computation.1 | async-start | bytes 262144 | tf_op jit(solution)/shard_map/all_to_all | solution.py:207
  92.5 0.9 select_reduce_fusion.1
  93.4 1.0 select_reduce_fusion
  94.4 0.9 fusion.7
  95.4 1.2 copy.57
  96.6 1.8 all-to-all-done.1
  98.3 3.5 %all-to-all-start.6 = ((bf16[512,4,128]{2,1,0:T(4,128)(2,1)}), bf16[512,4,128]{2,1,0:T(4,128)(2,1)S(1)}, u32[]{:S(2)}, u32[]{:S(2)}) async-start(bf16[512,4,128]{2,1,0:T(4,128)(2,1)} %copy.57), calls=%async_computation.6 | async-start | bytes 1048576 | tf_op jit(solution)/shard_map/all_to_all | solution.py:230
  101.8 3.9 %fusion.9 = (f32[4,512]{1,0:T(4,128)S(1)}, bf16[4,512,128]{2,1,0:T(8,128)(2,1)S(1)}) fusion(bf16[4,128,4,128]{3,1,0,2:T(8,128)(2,1)S(1)} %copy.51, bf16[512,128]{1,0:T(8,128)(2,1)S(1)} %bitcast.95, f32[4,512,512]{1,2,0:T(8,128)} %copy-done.1, f32[4,512]{1,0:T(4,128)S(1)} %log_add_fusion, pred[512,512]{0,1:T(8,128)(4,1)S(1)} %fusion.10), kind=kOutput, calls=%fused_computation.21 | convolution fusion | flops 273938432 | bytes 5652480 | tf_op jit(solution)/shard_map/while/body/eval_jaxpr/while/body/hqk,khd->qhd/dot_general | solution.py:102
  105.7 1.5 fusion
  107.2 0.7 fusion.5
  107.9 0.6 copy-done.4
  108.5 1.2 copy.55
  109.7 5.0 %all-to-all-done.6 = bf16[512,4,128]{2,1,0:T(4,128)(2,1)S(1)} async-done(((bf16[512,4,128]{2,1,0:T(4,128)(2,1)}), bf16[512,4,128]{2,1,0:T(4,128)(2,1)S(1)}, u32[]{:S(2)}, u32[]{:S(2)}) %all-to-all-start.6) | async-done | bytes 524320 | tf_op jit(solution)/shard_map/all_to_all | solution.py:230
  114.8 3.5 %all-to-all-start.5 = ((bf16[512,4,128]{2,1,0:T(4,128)(2,1)}), bf16[512,4,128]{2,1,0:T(4,128)(2,1)S(1)}, u32[]{:S(2)}, u32[]{:S(2)}) async-start(bf16[512,4,128]{2,1,0:T(4,128)(2,1)} %copy.55), calls=%async_computation.5 | async-start | bytes 1048576 | tf_op jit(solution)/shard_map/all_to_all | solution.py:229
  118.2 0.2 reduce-scatter.2.cloned.1.call-start
  118.5 0.7 reduce_sum.48
  119.3 12.1 %all-to-all-done.5 = bf16[512,4,128]{2,1,0:T(4,128)(2,1)S(1)} async-done(((bf16[512,4,128]{2,1,0:T(4,128)(2,1)}), bf16[512,4,128]{2,1,0:T(4,128)(2,1)S(1)}, u32[]{:S(2)}, u32[]{:S(2)}) %all-to-all-start.5) | async-done | bytes 524320 | tf_op jit(solution)/shard_map/all_to_all | solution.py:229
  131.4 0.7 reduce_sum.45
  132.2 3.2 %convert_bitcast_fusion = bf16[2048,1024]{0,1:T(8,128)(2,1)} fusion(bf16[1,128,2048]{2,1,0:T(8,128)(2,1)S(1)} %copy-done, bf16[128,512]{0,1:T(8,128)(2,1)S(1)} %bitcast.82, bf16[128,512]{0,1:T(8,128)(2,1)S(1)} %bitcast.84), kind=kOutput, calls=%fused_computation.2 | convolution fusion | flops 539492352 | bytes 4980736 | tf_op jit(solution)/shard_map/dot_general | solution.py:254
  135.4 1.2 copy.47
  136.6 3.5 %all-to-all-start.2 = ((bf16[512,4,128]{2,1,0:T(4,128)(2,1)}), bf16[512,4,128]{2,1,0:T(4,128)(2,1)S(1)}, u32[]{:S(2)}, u32[]{:S(2)}) async-start(bf16[512,4,128]{2,1,0:T(4,128)(2,1)} %copy.47), calls=%async_computation.2 | async-start | bytes 1048576 | tf_op jit(solution)/shard_map/all_to_all | solution.py:214
  140.1 2.6 %fusion.6 = bf16[512,4,128]{2,0,1:T(8,128)(2,1)S(1)} fusion(bf16[4,512,512]{1,2,0:T(8,128)(2,1)} %copy-done.4, bf16[512,128]{1,0:T(8,128)(2,1)S(1)} %bitcast.87), kind=kOutput, calls=%fused_computation.16 | convolution fusion | flops 268959744 | bytes 2752512 | tf_op jit(solution)/shard_map/while/body/eval_jaxpr/while/body/hqk,khd->qhd/dot_general | solution.py:154
  142.7 1.2 copy.53
  143.9 16.9 %all-to-all-done.2 = bf16[512,4,128]{2,1,0:T(4,128)(2,1)S(1)} async-done(((bf16[512,4,128]{2,1,0:T(4,128)(2,1)}), bf16[512,4,128]{2,1,0:T(4,128)(2,1)S(1)}, u32[]{:S(2)}, u32[]{:S(2)}) %all-to-all-start.2) | async-done | bytes 524320 | tf_op jit(solution)/shard_map/all_to_all | solution.py:214
  160.9 4.0 %all-to-all-start.4 = ((bf16[512,4,128]{2,1,0:T(4,128)(2,1)}), bf16[512,4,128]{2,1,0:T(4,128)(2,1)S(1)}, u32[]{:S(2)}, u32[]{:S(2)}) async-start(bf16[512,4,128]{2,1,0:T(4,128)(2,1)} %copy.53), calls=%async_computation.4 | async-start | bytes 1048576 | tf_op jit(solution)/shard_map/all_to_all | solution.py:228
  164.8 34.9 %reduce-scatter.2.cloned.1.call-done = bf16[256,1024]{0,1:T(8,128)(2,1)} async-done(((bf16[2048,1024]{0,1:T(8,128)(2,1)}), bf16[256,1024]{0,1:T(8,128)(2,1)}) %reduce-scatter.2.cloned.1.call-update) | async-done | bytes 524304 | tf_op jit(solution)/shard_map/reduce_scatter | solution.py:253
  199.9 1.2 reshape.239
  201.3 1.2 reshape.240
  202.5 4.5 %fusion.2 = bf16[1,128,2048]{2,1,0:T(8,128)(2,1)} fusion(bf16[2048,1024]{1,0:T(8,128)(2,1)} %all-gather.3.cloned.1.call-done, bf16[128,512]{0,1:T(8,128)(2,1)S(1)} %bitcast.83, bf16[128,512]{0,1:T(8,128)(2,1)S(1)} %bitcast.85), kind=kOutput, calls=%fused_computation.8 | convolution fusion | flops 537657344 | bytes 4980736 | tf_op jit(solution)/shard_map/dot_general | solution.py:245
  207.0 28.0 %all-reduce.2.cloned.1.call-done = bf16[256,1024]{0,1:T(8,128)(2,1)} async-done(((bf16[256,1024]{0,1:T(8,128)(2,1)}), bf16[256,1024]{0,1:T(8,128)(2,1)}) %all-reduce.2.cloned.1.call-update) | async-done | bytes 524304 | tf_op jit(solution)/shard_map/psum | solution.py:261
  235.0 1.1 fusion.22
  236.1 0.8 copy.60
  236.9 0.8 copy.59
  (32 shorter events, 1.4 us)
Async XLA Ops:
  7.2 66.7 %copy-start = (bf16[1,128,2048]{2,1,0:T(8,128)(2,1)S(1)}, bf16[1,128,2048]{2,1,0:T(8,128)(2,1)}, u32[]{:S(2)}) copy-start(bf16[1,128,2048]{2,1,0:T(8,128)(2,1)} %param.6) | copy-start | bytes 1572868
  7.2 15.9 %copy-start.3 = (s32[1,128]{1,0:T(1,128)S(1)}, s32[1,128]{1,0:T(1,128)}, u32[]{:S(2)}) copy-start(s32[1,128]{1,0:T(1,128)} %param.10) | copy-start | bytes 1540
  7.2 66.6 %all-gather.3.cloned.1.call-start = ((), (), s32[]{:S(2)}) async-start(), calls=%async_computation.8 | async-start | bytes 4718592 | tf_op jit(solution)/shard_map/all_gather | solution.py:191
  10.8 72.1 %collective-permute-start.2 = (bf16[1,128,4,128]{3,2,0,1:T(4,128)(2,1)S(1)}, bf16[1,128,4,128]{3,2,0,1:T(4,128)(2,1)S(1)}, u32[]{:S(2)}, u32[]{:S(2)}) collective-permute-start(bf16[1,128,4,128]{3,2,0,1:T(4,128)(2,1)S(1)} %get-tuple-element.282), channel_id=1, source_target_pairs={{0,12},{4,0},{8,4},{12,8},{1,13},{5,1},{9,5},{13,9},{2,14},{6,2},{... | collective-permute-start | bytes 393224 | tf_op jit(solution)/shard_map/ppermute | solution.py:34
  15.9 66.9 %collective-permute-start.1 = (bf16[1,128,4,128]{3,2,0,1:T(4,128)(2,1)S(1)}, bf16[1,128,4,128]{3,2,0,1:T(4,128)(2,1)S(1)}, u32[]{:S(2)}, u32[]{:S(2)}) collective-permute-start(bf16[1,128,4,128]{3,2,0,1:T(4,128)(2,1)S(1)} %get-tuple-element.283), channel_id=1, source_target_pairs={{0,8},{4,12},{8,0},{12,4},{1,9},{5,13},{9,1},{13,5},{2,10},{6,14},... | collective-permute-start | bytes 393224 | tf_op jit(solution)/shard_map/ppermute | solution.py:34
  15.9 35.6 %collective-permute-start = (bf16[1,128,4,128]{3,2,0,1:T(4,128)(2,1)S(1)}, bf16[1,128,4,128]{3,2,0,1:T(4,128)(2,1)S(1)}, u32[]{:S(2)}, u32[]{:S(2)}) collective-permute-start(bf16[1,128,4,128]{3,2,0,1:T(4,128)(2,1)S(1)} %get-tuple-element.284), channel_id=1, source_target_pairs={{0,4},{4,8},{8,12},{12,0},{1,5},{5,9},{9,13},{13,1},{2,6},{6,10},{... | collective-permute-start | bytes 393224 | tf_op jit(solution)/shard_map/ppermute | solution.py:34
  19.0 59.2 %all-to-all-start.3 = ((bf16[128,16,128]{0,2,1:T(8,128)(2,1)}), bf16[128,16,128]{0,2,1:T(8,128)(2,1)S(1)}, u32[]{:S(2)}, u32[]{:S(2)}) async-start(bf16[128,16,128]{0,2,1:T(8,128)(2,1)} %bitcast.21), calls=%async_computation.3 | async-start | bytes 1048576 | tf_op jit(solution)/shard_map/all_to_all | solution.py:217
  78.1 11.0 %all-to-all-start = ((bf16[128,4,128]{2,0,1:T(8,128)(2,1)}), bf16[128,4,128]{2,0,1:T(8,128)(2,1)S(1)}, u32[]{:S(2)}, u32[]{:S(2)}) async-start(bf16[128,4,128]{2,0,1:T(8,128)(2,1)} %copy.44), calls=%async_computation | async-start | bytes 262144 | tf_op jit(solution)/shard_map/all_to_all | solution.py:206
  89.1 9.2 %all-to-all-start.1 = ((bf16[128,4,128]{2,0,1:T(8,128)(2,1)}), bf16[128,4,128]{2,0,1:T(8,128)(2,1)S(1)}, u32[]{:S(2)}, u32[]{:S(2)}) async-start(bf16[128,4,128]{2,0,1:T(8,128)(2,1)} %copy.45), calls=%async_computation.1 | async-start | bytes 262144 | tf_op jit(solution)/shard_map/all_to_all | solution.py:207
  93.3 2.0 copy-start.1
  98.3 16.4 %all-to-all-start.6 = ((bf16[512,4,128]{2,1,0:T(4,128)(2,1)}), bf16[512,4,128]{2,1,0:T(4,128)(2,1)S(1)}, u32[]{:S(2)}, u32[]{:S(2)}) async-start(bf16[512,4,128]{2,1,0:T(4,128)(2,1)} %copy.57), calls=%async_computation.6 | async-start | bytes 1048576 | tf_op jit(solution)/shard_map/all_to_all | solution.py:230
  101.8 3.9 %copy-start.2 = (f32[4,512,512]{1,2,0:T(8,128)S(1)}, f32[4,512,512]{1,2,0:T(8,128)}, u32[]{:S(2)}) copy-start(f32[4,512,512]{1,2,0:T(8,128)} %copy-done.1) | copy-start | bytes 12582916
  107.2 1.4 copy-start.4
  114.8 16.6 %all-to-all-start.5 = ((bf16[512,4,128]{2,1,0:T(4,128)(2,1)}), bf16[512,4,128]{2,1,0:T(4,128)(2,1)S(1)}, u32[]{:S(2)}, u32[]{:S(2)}) async-start(bf16[512,4,128]{2,1,0:T(4,128)(2,1)} %copy.55), calls=%async_computation.5 | async-start | bytes 1048576 | tf_op jit(solution)/shard_map/all_to_all | solution.py:229
  118.2 81.5 %reduce-scatter.2.cloned.1.call-start = ((), (), s32[]{:S(2)}) async-start(), calls=%async_computation.9 | async-start | bytes 4718592 | tf_op jit(solution)/shard_map/reduce_scatter | solution.py:253
  136.6 24.3 %all-to-all-start.2 = ((bf16[512,4,128]{2,1,0:T(4,128)(2,1)}), bf16[512,4,128]{2,1,0:T(4,128)(2,1)S(1)}, u32[]{:S(2)}, u32[]{:S(2)}) async-start(bf16[512,4,128]{2,1,0:T(4,128)(2,1)} %copy.47), calls=%async_computation.2 | async-start | bytes 1048576 | tf_op jit(solution)/shard_map/all_to_all | solution.py:214
  160.9 40.3 %all-to-all-start.4 = ((bf16[512,4,128]{2,1,0:T(4,128)(2,1)}), bf16[512,4,128]{2,1,0:T(4,128)(2,1)S(1)}, u32[]{:S(2)}, u32[]{:S(2)}) async-start(bf16[512,4,128]{2,1,0:T(4,128)(2,1)} %copy.53), calls=%async_computation.4 | async-start | bytes 1048576 | tf_op jit(solution)/shard_map/all_to_all | solution.py:228
  164.8 70.2 %all-reduce.2.cloned.1.call-start = ((), (), s32[]{:S(2)}) async-start(), calls=%async_computation.10 | async-start | bytes 1048576 | tf_op jit(solution)/shard_map/psum | solution.py:261
Sparse Core Ops, SparseCore 0:
  10.2 63.5 all-gather.2
  135.5 64.1 reduce-scatter.1
  202.0 32.9 all-reduce.1
